TPU v7x, 512 devices: a whole 4x4x16 slice. The times are simulated.
512 devices in a mesh: pipe: 8 (over x, core), expert: 64 (over z, y).
Axes of the slice: x: 4, y: 4, z: 16, core: 2. Of those that a mesh axis runs over, the one named last changes fastest.
Arguments:
- inputs: bfloat16 [8, 8192, 2048], P('pipe', 'expert'), may hold values from -6 to 6
- out_grads: bfloat16 [8, 8192, 2048], P('pipe', 'expert'), may hold values from -6 to 6
- expert_ids: int32 [8, 8192, 8], P('pipe', 'expert'), may hold values from 0 to 127, all different within a row
- gate_values: float32 [8, 8192, 8], P('pipe', 'expert'), may hold values from 0.2 to 1
- w_gate: bfloat16 [8, 2048, 16384], P('pipe', None, 'expert'), may hold values from -0.125 to 0.125
- w_up: bfloat16 [8, 2048, 16384], P('pipe', None, 'expert'), may hold values from -0.125 to 0.125
- w_down: bfloat16 [8, 16384, 2048], P('pipe', 'expert'), may hold values from -0.1875 to 0.1875
Outputs:
- prev_grads: bfloat16 [8, 8192, 2048], P('pipe', 'expert')
- gate_grads: float32 [8, 8192, 8], P('pipe', 'expert')
Inputs may be any that keep to these rules, and one draw needn't show every extreme that they name: `expert_ids`: each token names 8 different experts.
All inputs are finite; a program needn't handle non-finite values.
Results may differ from a plain program's by a relative error of at most 0.0057.
Values may be sent and summed in bfloat16 or wider, within the bound.
A program may use at most 64 MiB of HBM per device.

v0:
```python
import jax
import jax.numpy as jnp
from jax import lax
from jax.sharding import PartitionSpec as P

SLICES = 4
CAP = 12


def shifted(block, axis, distance):
    devices = range(lax.axis_size(axis))
    route = [((i - distance) % len(devices), i) for i in devices]
    return lax.ppermute(block, axis, route)


def expert_grads(rows_in, rows_grad, gate_cols, up_cols, down_rows):
    gate_pre = jnp.dot(rows_in, gate_cols, preferred_element_type=jnp.float32)
    up_pre = jnp.dot(rows_in, up_cols, preferred_element_type=jnp.float32)
    sig = jax.nn.sigmoid(gate_pre)
    act = gate_pre * sig
    hidden = act * up_pre
    dhidden = lax.dot_general(
        rows_grad, down_rows, (((1,), (1,)), ((), ())), preferred_element_type=jnp.float32
    )
    gate_part = jnp.sum(hidden * dhidden, axis=1)
    d_gate_pre = (dhidden * up_pre * sig * (1.0 + gate_pre * (1.0 - sig))).astype(jnp.bfloat16)
    d_up_pre = (dhidden * act).astype(jnp.bfloat16)
    back = lax.dot_general(
        d_gate_pre, gate_cols, (((1,), (1,)), ((), ())), preferred_element_type=jnp.float32
    )
    back = back + lax.dot_general(
        d_up_pre, up_cols, (((1,), (1,)), ((), ())), preferred_element_type=jnp.float32
    )
    return (back, gate_part)


def send_back(back, gate_part):
    return (
        lax.all_to_all(back, "expert", split_axis=0, concat_axis=0, tiled=True),
        lax.all_to_all(gate_part, "expert", split_axis=0, concat_axis=0, tiled=True),
    )


def per_device(inputs, out_grads, expert_ids, gate_values, w_gate, w_up, w_down):
    devices_axis = lax.axis_size("expert")
    flight = devices_axis // SLICES
    tokens = inputs[0]
    grads = out_grads[0]
    ids = expert_ids[0]
    gates = gate_values[0]
    gate_cols = w_gate[0]
    up_cols = w_up[0]
    down_rows = w_down[0]
    count = tokens.shape[0]
    width = tokens.shape[1]
    experts_here = jnp.arange(flight, dtype=jnp.int32)
    match = ids[:, :, None] == experts_here[None, None, :]
    routed = jnp.sum(match.astype(jnp.int32), axis=1)
    weight_te = jnp.sum(jnp.where(match, gates[:, :, None], jnp.float32(0.0)), axis=1)
    before = jnp.cumsum(routed, axis=0) - routed
    kept = (routed > 0) & (before < CAP)
    slots = jnp.arange(CAP, dtype=jnp.int32)
    place = kept.T[:, None, :] & (before.T[:, None, :] == slots[None, :, None])
    place_bf = place.astype(jnp.bfloat16)
    send_x = jnp.einsum("ect,td->ecd", place_bf, tokens, preferred_element_type=jnp.float32).astype(
        jnp.bfloat16
    )
    send_g = jnp.einsum("ect,td->ecd", place_bf, grads, preferred_element_type=jnp.float32).astype(
        jnp.bfloat16
    )
    send_x = jnp.broadcast_to(send_x[:, None], (flight, SLICES, CAP, width)).reshape(
        devices_axis, CAP, width
    )
    send_g = jnp.broadcast_to(send_g[:, None], (flight, SLICES, CAP, width)).reshape(
        devices_axis, CAP, width
    )
    rows_in = lax.all_to_all(send_x, "expert", split_axis=0, concat_axis=0, tiled=True)
    rows_grad = lax.all_to_all(send_g, "expert", split_axis=0, concat_axis=0, tiled=True)
    lead = rows_in.shape[0]
    items = rows_in.shape[1]
    back, part = expert_grads(
        rows_in.reshape(lead * items, width),
        rows_grad.reshape(lead * items, width),
        gate_cols,
        up_cols,
        down_rows,
    )
    back_bf = back.astype(jnp.bfloat16).reshape(lead, items, width)
    part_bf = part.astype(jnp.bfloat16).reshape(lead, items)
    received, gate_back = send_back(back_bf, part_bf)
    total = jnp.sum(received.astype(jnp.float32).reshape(flight, SLICES, CAP, width), axis=1)
    gsum = jnp.sum(gate_back.astype(jnp.float32).reshape(flight, SLICES, CAP), axis=1)
    place_f = place.astype(jnp.float32)
    mix = jnp.transpose(place_f * weight_te.T[:, None, :], (2, 0, 1)).reshape(count, flight * CAP)
    moe = jnp.dot(
        mix,
        total.reshape(flight * CAP, width),
        precision=lax.Precision.HIGHEST,
        preferred_element_type=jnp.float32,
    )
    moe_bf = moe.astype(jnp.bfloat16)
    d_gate_te = jnp.einsum("ect,ec->te", place_f, gsum, precision=lax.Precision.HIGHEST)
    d_gates = jnp.sum(jnp.where(match, d_gate_te[:, None, :], jnp.float32(0.0)), axis=2)
    arrived = shifted(moe_bf, "pipe", -1)
    return (arrived[None], d_gates[None])


def solution(mesh):
    return jax.shard_map(
        per_device,
        mesh=mesh,
        in_specs=(
            P("pipe", "expert", None),
            P("pipe", "expert", None),
            P("pipe", "expert", None),
            P("pipe", "expert", None),
            P("pipe", None, "expert"),
            P("pipe", None, "expert"),
            P("pipe", "expert", None),
        ),
        out_specs=(P("pipe", "expert", None), P("pipe", "expert", None)),
        check_vma=False,
    )
```

profile of v0, /device:TPU:1, one launch (start us, length us, event | category | flops | bytes accessed | tf_op | source)
XLA Modules:
  0.0 664.8 jit_solution(15382559104927822747)
XLA Ops:
  0.6 0.0 copy-start
  0.6 0.8 convert_reduce_fusion.1
  1.4 0.1 copy.46
  1.5 0.2 reduce_window_sum.11
  1.7 0.1 copy.47
  1.8 1.4 convolution_convert_fusion
  3.2 0.4 copy.49
  3.7 2.5 broadcast_in_dim.52
  6.1 0.0 copy-start.3
  6.1 19.7 %all-to-all-start.1 = ((bf16[64,12,2048]{2,1,0:T(8,128)(2,1)}), bf16[64,12,2048]{2,1,0:T(8,128)(2,1)}, u32[]{:S(2)}, u32[]{:S(2)}) async-start(bf16[64,12,2048]{2,1,0:T(8,128)(2,1)} %bitcast.53), calls=%async_computation.1 | async-start | bytes 8388608 | tf_op jit(solution)/shard_map/all_to_all | solution.py:77
  25.8 0.0 copy-done.3
  25.8 0.4 convolution_convert_fusion.1
  26.2 0.5 copy.48
  26.6 182.8 %all-to-all-done.1 = bf16[64,12,2048]{2,1,0:T(8,128)(2,1)} async-done(((bf16[64,12,2048]{2,1,0:T(8,128)(2,1)}), bf16[64,12,2048]{2,1,0:T(8,128)(2,1)}, u32[]{:S(2)}, u32[]{:S(2)}) %all-to-all-start.1) | async-done | bytes 3145760 | tf_op jit(solution)/shard_map/all_to_all | solution.py:77
  209.4 2.5 broadcast_in_dim.51
  211.9 11.9 %all-to-all-start = ((bf16[64,12,2048]{2,1,0:T(8,128)(2,1)}), bf16[64,12,2048]{2,1,0:T(8,128)(2,1)}, u32[]{:S(2)}, u32[]{:S(2)}) async-start(bf16[64,12,2048]{2,1,0:T(8,128)(2,1)} %bitcast.52), calls=%async_computation | async-start | bytes 8388608 | tf_op jit(solution)/shard_map/all_to_all | solution.py:78
  223.9 6.2 reshape.57
  230.0 0.0 copy-done
  230.0 0.0 copy-start.1
  230.0 0.0 copy-start.2
  230.0 3.1 fusion.4
  233.1 0.0 copy-done.1
  233.1 0.0 copy-done.2
  233.1 1.1 fusion.7
  234.2 173.2 %all-to-all-done = bf16[64,12,2048]{2,1,0:T(8,128)(2,1)} async-done(((bf16[64,12,2048]{2,1,0:T(8,128)(2,1)}), bf16[64,12,2048]{2,1,0:T(8,128)(2,1)}, u32[]{:S(2)}, u32[]{:S(2)}) %all-to-all-start) | async-done | bytes 3145760 | tf_op jit(solution)/shard_map/all_to_all | solution.py:78
  407.5 6.2 reshape.55
  413.6 3.2 multiply_reduce_fusion
  416.9 3.9 fusion.2
  420.8 0.7 convert_element_type.61
  421.5 11.4 %all-to-all-start.3 = ((bf16[64,1,12]{2,1,0:T(2,128)(2,1)}), bf16[64,1,12]{2,1,0:T(2,128)(2,1)S(1)}, u32[]{:S(2)}, u32[]{:S(2)}) async-start(bf16[64,1,12]{2,1,0:T(2,128)(2,1)} %convert_element_type.61), calls=%async_computation.3 | async-start | bytes 65536 | tf_op jit(solution)/shard_map/all_to_all | solution.py:40
  432.9 5.9 add_convert_fusion
  438.8 6.1 reshape.58
  444.9 0.0 copy-start.4
  444.9 0.0 copy-start.5
  444.9 1.4 all-to-all-done.3
  446.3 13.5 %all-to-all-start.2 = ((bf16[64,12,2048]{2,1,0:T(8,128)(2,1)}), bf16[64,12,2048]{2,1,0:T(8,128)(2,1)}, u32[]{:S(2)}, u32[]{:S(2)}) async-start(bf16[64,12,2048]{2,1,0:T(8,128)(2,1)} %reshape.58), calls=%async_computation.2 | async-start | bytes 8388608 | tf_op jit(solution)/shard_map/all_to_all | solution.py:39
  459.9 0.2 fusion.16
  460.1 0.0 copy-done.4
  460.1 0.0 copy-done.5
  460.2 0.6 select_reduce_fusion
  460.8 181.5 %all-to-all-done.2 = bf16[64,12,2048]{2,1,0:T(8,128)(2,1)} async-done(((bf16[64,12,2048]{2,1,0:T(8,128)(2,1)}), bf16[64,12,2048]{2,1,0:T(8,128)(2,1)}, u32[]{:S(2)}, u32[]{:S(2)}) %all-to-all-start.2) | async-done | bytes 3145760 | tf_op jit(solution)/shard_map/all_to_all | solution.py:39
  642.3 3.3 convert_reduce_fusion
  645.6 2.0 fusion
  647.6 8.4 %collective-permute-start = (bf16[128,2048]{1,0:T(8,128)(2,1)S(1)}, bf16[128,2048]{1,0:T(8,128)(2,1)S(1)}, u32[]{:S(2)}, u32[]{:S(2)}) collective-permute-start(bf16[128,2048]{1,0:T(8,128)(2,1)S(1)} %fusion), channel_id=1, source_target_pairs={{64,0},{128,64},{192,128},{256,192},{320,256},{384,320},{448,384},... | collective-permute-start | bytes 1572872 | tf_op jit(solution)/shard_map/ppermute | solution.py:13
  656.0 8.0 %collective-permute-done = bf16[128,2048]{1,0:T(8,128)(2,1)S(1)} collective-permute-done((bf16[128,2048]{1,0:T(8,128)(2,1)S(1)}, bf16[128,2048]{1,0:T(8,128)(2,1)S(1)}, u32[]{:S(2)}, u32[]{:S(2)}) %collective-permute-start) | collective-permute-done | bytes 524320 | tf_op jit(solution)/shard_map/ppermute | solution.py:13
  664.0 0.8 copy.60
  (5 shorter events, 0.1 us)
Async XLA Ops:
  0.6 229.4 %copy-start = (bf16[1,2048,256]{2,1,0:T(8,128)(2,1)S(1)}, bf16[1,2048,256]{2,1,0:T(8,128)(2,1)}, u32[]{:S(2)}) copy-start(bf16[1,2048,256]{2,1,0:T(8,128)(2,1)} %param.11) | copy-start | bytes 3145732
  6.1 19.7 %copy-start.3 = (bf16[1,128,2048]{2,1,0:T(8,128)(2,1)S(1)}, bf16[1,128,2048]{2,1,0:T(8,128)(2,1)}, u32[]{:S(2)}) copy-start(bf16[1,128,2048]{2,1,0:T(8,128)(2,1)} %param.8) | copy-start | bytes 1572868
  6.1 203.3 %all-to-all-start.1 = ((bf16[64,12,2048]{2,1,0:T(8,128)(2,1)}), bf16[64,12,2048]{2,1,0:T(8,128)(2,1)}, u32[]{:S(2)}, u32[]{:S(2)}) async-start(bf16[64,12,2048]{2,1,0:T(8,128)(2,1)} %bitcast.53), calls=%async_computation.1 | async-start | bytes 8388608 | tf_op jit(solution)/shard_map/all_to_all | solution.py:77
  211.9 195.6 %all-to-all-start = ((bf16[64,12,2048]{2,1,0:T(8,128)(2,1)}), bf16[64,12,2048]{2,1,0:T(8,128)(2,1)}, u32[]{:S(2)}, u32[]{:S(2)}) async-start(bf16[64,12,2048]{2,1,0:T(8,128)(2,1)} %bitcast.52), calls=%async_computation | async-start | bytes 8388608 | tf_op jit(solution)/shard_map/all_to_all | solution.py:78
  230.0 3.1 copy-start.1
  230.0 3.1 copy-start.2
  421.5 24.8 %all-to-all-start.3 = ((bf16[64,1,12]{2,1,0:T(2,128)(2,1)}), bf16[64,1,12]{2,1,0:T(2,128)(2,1)S(1)}, u32[]{:S(2)}, u32[]{:S(2)}) async-start(bf16[64,1,12]{2,1,0:T(2,128)(2,1)} %convert_element_type.61), calls=%async_computation.3 | async-start | bytes 65536 | tf_op jit(solution)/shard_map/all_to_all | solution.py:40
  444.9 15.3 %copy-start.4 = (s32[1,128,8]{1,2,0:T(8,128)S(1)}, s32[1,128,8]{1,2,0:T(8,128)}, u32[]{:S(2)}) copy-start(s32[1,128,8]{1,2,0:T(8,128)} %param.9) | copy-start | bytes 12292
  444.9 15.3 %copy-start.5 = (f32[1,128,8]{1,2,0:T(8,128)S(1)}, f32[1,128,8]{1,2,0:T(8,128)}, u32[]{:S(2)}) copy-start(f32[1,128,8]{1,2,0:T(8,128)} %param.10) | copy-start | bytes 12292
  446.3 196.0 %all-to-all-start.2 = ((bf16[64,12,2048]{2,1,0:T(8,128)(2,1)}), bf16[64,12,2048]{2,1,0:T(8,128)(2,1)}, u32[]{:S(2)}, u32[]{:S(2)}) async-start(bf16[64,12,2048]{2,1,0:T(8,128)(2,1)} %reshape.58), calls=%async_computation.2 | async-start | bytes 8388608 | tf_op jit(solution)/shard_map/all_to_all | solution.py:39
  647.6 16.4 %collective-permute-start = (bf16[128,2048]{1,0:T(8,128)(2,1)S(1)}, bf16[128,2048]{1,0:T(8,128)(2,1)S(1)}, u32[]{:S(2)}, u32[]{:S(2)}) collective-permute-start(bf16[128,2048]{1,0:T(8,128)(2,1)S(1)} %fusion), channel_id=1, source_target_pairs={{64,0},{128,64},{192,128},{256,192},{320,256},{384,320},{448,384},... | collective-permute-start | bytes 1572872 | tf_op jit(solution)/shard_map/ppermute | solution.py:13
where the time goes:
time: 666 us; the launch traced here: 665 us
  waiting for transfers between devices  547 us (82%)
  starting transfers between devices  64.9 us (10%)
  local copies, waits for them, and re-layouts  26 us (4%)
  matrix products  21.1 us (3%)
    all_to_all x1, waiting for transfers between devices, per_device(): lax.all_to_all(send_x, 'expert', split_axis=0, concat_axis=0, tiled=True)  183 us
    all_to_all x1, waiting for transfers between devices, send_back(): lax.all_to_all(back, 'expert', split_axis=0, concat_axis=0, tiled=True)  182 us
    all_to_all x1, waiting for transfers between devices, per_device(): lax.all_to_all(send_g, 'expert', split_axis=0, concat_axis=0, tiled=True)  173 us
    all_to_all x1, starting transfers between devices, per_device(): lax.all_to_all(send_x, 'expert', split_axis=0, concat_axis=0, tiled=True)  19.7 us
    all_to_all x1, starting transfers between devices, send_back(): lax.all_to_all(back, 'expert', split_axis=0, concat_axis=0, tiled=True)  13.5 us
  transfers between devices with their start and end apart: 5, of which 5 were waited for; matrix products, arithmetic and copies ran while one was open for 4% of the time, Pallas kernels for 0%

commit v1 on v0

--- a/solution.py
+++ b/solution.py
@@ -34,10 +34,19 @@
     return (back, gate_part)
 
 
-def send_back(back, gate_part):
-    return (
-        lax.all_to_all(back, "expert", split_axis=0, concat_axis=0, tiled=True),
-        lax.all_to_all(gate_part, "expert", split_axis=0, concat_axis=0, tiled=True),
+def along_z():
+    planes = lax.axis_size("expert") // SLICES
+    return [[z * SLICES + y for z in range(planes)] for y in range(SLICES)]
+
+
+def along_y():
+    planes = lax.axis_size("expert") // SLICES
+    return [[z * SLICES + y for y in range(SLICES)] for z in range(planes)]
+
+
+def swap(block, groups):
+    return lax.all_to_all(
+        block, "expert", split_axis=0, concat_axis=0, tiled=True, axis_index_groups=groups
     )
 
 
@@ -68,28 +77,25 @@
     send_g = jnp.einsum("ect,td->ecd", place_bf, grads, preferred_element_type=jnp.float32).astype(
         jnp.bfloat16
     )
-    send_x = jnp.broadcast_to(send_x[:, None], (flight, SLICES, CAP, width)).reshape(
-        devices_axis, CAP, width
-    )
-    send_g = jnp.broadcast_to(send_g[:, None], (flight, SLICES, CAP, width)).reshape(
-        devices_axis, CAP, width
-    )
-    rows_in = lax.all_to_all(send_x, "expert", split_axis=0, concat_axis=0, tiled=True)
-    rows_grad = lax.all_to_all(send_g, "expert", split_axis=0, concat_axis=0, tiled=True)
-    lead = rows_in.shape[0]
-    items = rows_in.shape[1]
+    send = jnp.concatenate([send_x, send_g], axis=1)
+    mine = swap(send, along_z())
+    rows = lax.all_gather(mine, "expert", axis_index_groups=along_y(), axis=0, tiled=False)
+    rows = rows.reshape(devices_axis, 2 * CAP, width)
     back, part = expert_grads(
-        rows_in.reshape(lead * items, width),
-        rows_grad.reshape(lead * items, width),
+        rows[:, :CAP].reshape(devices_axis * CAP, width),
+        rows[:, CAP:].reshape(devices_axis * CAP, width),
         gate_cols,
         up_cols,
         down_rows,
     )
-    back_bf = back.astype(jnp.bfloat16).reshape(lead, items, width)
-    part_bf = part.astype(jnp.bfloat16).reshape(lead, items)
-    received, gate_back = send_back(back_bf, part_bf)
-    total = jnp.sum(received.astype(jnp.float32).reshape(flight, SLICES, CAP, width), axis=1)
-    gsum = jnp.sum(gate_back.astype(jnp.float32).reshape(flight, SLICES, CAP), axis=1)
+    back_bf = back.astype(jnp.bfloat16).reshape(SLICES, flight * CAP, width)
+    part_bf = part.astype(jnp.bfloat16).reshape(SLICES, flight * CAP)
+    parts = swap(back_bf, along_y())
+    qparts = swap(part_bf, along_y())
+    summed = jnp.sum(parts.astype(jnp.float32), axis=0).astype(jnp.bfloat16)
+    qsum = jnp.sum(qparts.astype(jnp.float32), axis=0)
+    total = swap(summed.reshape(flight, CAP, width), along_z()).astype(jnp.float32)
+    gsum = swap(qsum.reshape(flight, CAP), along_z())
     place_f = place.astype(jnp.float32)
     mix = jnp.transpose(place_f * weight_te.T[:, None, :], (2, 0, 1)).reshape(count, flight * CAP)
     moe = jnp.dot(

time: 666 us -> 347 us (0.52)
  waiting for transfers between devices: 547 us -> 170 us
  blocking collectives: 0 us -> 83.6 us
  starting transfers between devices: 64.9 us -> 29.6 us
  between operations: 0.83 us -> 14.2 us
    all_to_all x4, waiting for transfers between devices: 539 us -> 86.6 us  [swap(): lax.all_to_all(block, 'expert', split_axis=0, concat_axis=0, tiled=True,...]
    all_to_all x0 -> x1, blocking collectives: none -> 83.6 us  [swap(): lax.all_to_all(block, 'expert', split_axis=0, concat_axis=0, tiled=True,...]
    all_gather x0 -> x1, waiting for transfers between devices: none -> 75.2 us  [per_device(): lax.all_gather(mine, 'expert', axis_index_groups=along_y(), axis=0, tiled...]
    all_to_all x4, starting transfers between devices: 56.5 us -> 24 us  [swap(): lax.all_to_all(block, 'expert', split_axis=0, concat_axis=0, tiled=True,...]
    slice x0 -> x1, local copies, waits for them, and re-layouts: none -> 6.66 us  [per_device(): rows[:, CAP:].reshape(devices_axis * CAP, width)]
  transfers between devices with their start and end apart: 5 -> 6, of which waited for: 5 -> 5; matrix products, arithmetic and copies ran while one was open for 4% -> 3% of each run, Pallas kernels for 0% -> 0%
where the time goes in v1:
time: 347 us; the launch traced here: 346 us
  waiting for transfers between devices  170 us (49%)
  blocking collectives  83.6 us (24%)
  starting transfers between devices  29.6 us (9%)
  local copies, waits for them, and re-layouts  23.4 us (7%)
  matrix products  21.1 us (6%)
  between operations  14.2 us (4%)
  other arithmetic  4.34 us (1%)
    all_to_all x4, waiting for transfers between devices, swap(): lax.all_to_all(block, 'expert', split_axis=0, concat_axis=0, tiled=True,...  86.6 us
    all_to_all x1, blocking collectives, swap(): lax.all_to_all(block, 'expert', split_axis=0, concat_axis=0, tiled=True,...  83.6 us
    all_gather x1, waiting for transfers between devices, per_device(): lax.all_gather(mine, 'expert', axis_index_groups=along_y(), axis=0, tiled...  75.2 us
    all_to_all x4, starting transfers between devices, swap(): lax.all_to_all(block, 'expert', split_axis=0, concat_axis=0, tiled=True,...  24 us
    ppermute x1, waiting for transfers between devices, shifted(): return lax.ppermute(block, axis, route)  7.93 us
  transfers between devices with their start and end apart: 6, of which 5 were waited for; matrix products, arithmetic and copies ran while one was open for 3% of the time, Pallas kernels for 0%

profile of v1, /device:TPU:1, one launch (start us, length us, event | category | flops | bytes accessed | tf_op | source)
XLA Modules:
  0.0 346.1 jit_solution(2101810319506277899)
XLA Ops:
  7.2 0.0 copy-start
  7.2 0.0 all-gather.3.cloned.1.call-start
  7.2 0.8 convert_reduce_fusion
  8.0 0.1 copy.55
  8.1 0.2 reduce_window_sum.11
  8.3 0.1 copy.56
  8.4 1.4 convolution_convert_fusion.1
  9.8 1.4 convolution_convert_fusion
  11.2 0.1 pad_maximum_fusion
  11.3 0.9 copy.57
  12.2 83.6 %all_to_all.33 = bf16[16,24,2048]{2,1,0:T(8,128)(2,1)} all-to-all(bf16[16,24,2048]{2,1,0:T(8,128)(2,1)S(1)} %copy.57), channel_id=1, replica_groups={{0,4,8,12,16,20,24,28,32,36,40,44,48,52,56,60},{1,5,9,13,17,21,25,29,33..., dimensions={0} | all-to-all | bytes 3145728 | tf_op jit(solution)/shard_map/all_to_all | solution.py:48
  95.8 0.0 all-gather.3.cloned.1.call-update
  95.8 75.2 %all-gather.3.cloned.1.call-done = bf16[64,24,2048]{2,1,0:T(8,128)(2,1)} async-done(((bf16[16,24,2048]{2,1,0:T(8,128)(2,1)}), bf16[64,24,2048]{2,1,0:T(8,128)(2,1)}) %all-gather.3.cloned.1.call-update) | async-done | bytes 6291472 | tf_op jit(solution)/shard_map/all_gather | solution.py:82
  171.1 6.7 %fusion.32 = (bf16[64,12,2048]{2,1,0:T(8,128)(2,1)}, bf16[64,12,2048]{2,1,0:T(8,128)(2,1)}) fusion(bf16[64,24,2048]{2,1,0:T(8,128)(2,1)} %all-gather.3.cloned.1.call-done), kind=kLoop, calls=%fused_computation.47 | loop fusion | bytes 12582912 | tf_op jit(solution)/shard_map/slice | solution.py:86
  177.7 6.2 %reshape.49 = bf16[768,2048]{1,0:T(8,128)(2,1)} reshape(bf16[64,12,2048]{2,1,0:T(8,128)(2,1)} %get-tuple-element.8) | data formatting | bytes 6291456 | tf_op jit(solution)/shard_map/reshape | solution.py:85
  183.9 0.0 copy-done
  183.9 0.0 copy-start.1
  183.9 0.0 copy-start.2
  183.9 3.1 fusion.3
  187.0 0.0 copy-done.1
  187.0 0.0 copy-done.2
  187.0 1.1 fusion.6
  188.1 6.2 %reshape.48 = bf16[768,2048]{1,0:T(8,128)(2,1)} reshape(bf16[64,12,2048]{2,1,0:T(8,128)(2,1)} %get-tuple-element.7) | data formatting | bytes 6291456 | tf_op jit(solution)/shard_map/reshape | solution.py:86
  194.3 3.2 multiply_reduce_fusion
  197.6 3.9 %fusion.1 = f32[768,2048]{1,0:T(8,128)} fusion(bf16[1,2048,256]{2,1,0:T(8,128)(2,1)S(1)} %copy-done, f32[768,256]{0,1:T(8,128)S(1)} %fusion.3, f32[768,256]{0,1:T(8,128)S(1)} %get-tuple-element.10, f32[768,256]{0,1:T(8,128)S(1)} %fusion.6), kind=kOutput, calls=%fused_computation.6 | convolution fusion | flops 807272448 | bytes 9699328 | tf_op jit(solution)/shard_map/dot_general | solution.py:28
  201.5 0.7 convert_element_type.54
  202.2 3.4 all-to-all-start.3
  205.5 5.9 %add_convert_fusion = bf16[768,2048]{1,0:T(8,128)(2,1)} fusion(f32[768,2048]{1,0:T(8,128)} %fusion.1, bf16[1,2048,256]{2,1,0:T(8,128)(2,1)} %param.12, f32[768,256]{0,1:T(8,128)S(1)} %get-tuple-element.10, f32[768,256]{0,1:T(8,128)S(1)} %fusion.3), kind=kOutput, calls=%fused_computation | convolution fusion | flops 809631744 | bytes 12058624 | tf_op jit(solution)/shard_map/dot_general | solution.py:31
  211.4 0.0 all-to-all-done.3
  211.4 4.6 %all-to-all-start.1 = ((bf16[4,192,2048]{2,1,0:T(8,128)(2,1)}), bf16[4,192,2048]{2,1,0:T(8,128)(2,1)}, u32[]{:S(2)}, u32[]{:S(2)}) async-start(bf16[4,192,2048]{2,1,0:T(8,128)(2,1)} %bitcast.50), calls=%async_computation.1 | async-start | bytes 6291456 | tf_op jit(solution)/shard_map/all_to_all | solution.py:48
  216.1 0.7 all_to_all.25
  216.8 35.7 %all-to-all-done.1 = bf16[4,192,2048]{2,1,0:T(8,128)(2,1)} async-done(((bf16[4,192,2048]{2,1,0:T(8,128)(2,1)}), bf16[4,192,2048]{2,1,0:T(8,128)(2,1)}, u32[]{:S(2)}, u32[]{:S(2)}) %all-to-all-start.1) | async-done | bytes 3145760 | tf_op jit(solution)/shard_map/all_to_all | solution.py:48
  252.5 12.0 %all-to-all-start.4 = ((f32[16,1,12]{2,1,0:T(1,128)}), f32[16,1,12]{2,1,0:T(1,128)S(1)}, u32[]{:S(2)}, u32[]{:S(2)}) async-start(f32[16,1,12]{2,1,0:T(1,128)} %bitcast.14), calls=%async_computation.4 | async-start | bytes 16384 | tf_op jit(solution)/shard_map/all_to_all | solution.py:48
  264.5 0.0 copy-start.3
  264.5 0.0 copy-start.4
  264.6 2.6 reduce_sum.59
  267.1 1.2 reshape.51
  268.3 7.5 %all-to-all-done.4 = f32[16,1,12]{2,1,0:T(1,128)S(1)} async-done(((f32[16,1,12]{2,1,0:T(1,128)}), f32[16,1,12]{2,1,0:T(1,128)S(1)}, u32[]{:S(2)}, u32[]{:S(2)}) %all-to-all-start.4) | async-done | bytes 800 | tf_op jit(solution)/shard_map/all_to_all | solution.py:48
  275.8 4.0 %all-to-all-start.2 = ((bf16[16,12,2048]{2,1,0:T(8,128)(2,1)}), bf16[16,12,2048]{2,1,0:T(8,128)(2,1)S(1)}, u32[]{:S(2)}, u32[]{:S(2)}) async-start(bf16[16,12,2048]{2,1,0:T(8,128)(2,1)} %reshape.51), calls=%async_computation.2 | async-start | bytes 2097152 | tf_op jit(solution)/shard_map/all_to_all | solution.py:48
  279.8 0.2 fusion.16
  280.0 0.0 copy-done.3
  280.0 0.0 copy-done.4
  280.0 0.6 select_reduce_fusion
  280.6 43.3 %all-to-all-done.2 = bf16[16,12,2048]{2,1,0:T(8,128)(2,1)S(1)} async-done(((bf16[16,12,2048]{2,1,0:T(8,128)(2,1)}), bf16[16,12,2048]{2,1,0:T(8,128)(2,1)S(1)}, u32[]{:S(2)}, u32[]{:S(2)}) %all-to-all-start.2) | async-done | bytes 786464 | tf_op jit(solution)/shard_map/all_to_all | solution.py:48
  323.9 1.0 fusion
  324.9 5.6 %collective-permute-start = (bf16[128,2048]{1,0:T(8,128)(2,1)S(1)}, bf16[128,2048]{1,0:T(8,128)(2,1)S(1)}, u32[]{:S(2)}, u32[]{:S(2)}) collective-permute-start(bf16[128,2048]{1,0:T(8,128)(2,1)S(1)} %fusion), channel_id=1, source_target_pairs={{64,0},{128,64},{192,128},{256,192},{320,256},{384,320},{448,384},... | collective-permute-start | bytes 1572872 | tf_op jit(solution)/shard_map/ppermute | solution.py:13
  330.5 7.9 %collective-permute-done = bf16[128,2048]{1,0:T(8,128)(2,1)S(1)} collective-permute-done((bf16[128,2048]{1,0:T(8,128)(2,1)S(1)}, bf16[128,2048]{1,0:T(8,128)(2,1)S(1)}, u32[]{:S(2)}, u32[]{:S(2)}) %collective-permute-start) | collective-permute-done | bytes 524320 | tf_op jit(solution)/shard_map/ppermute | solution.py:13
  338.4 0.8 copy.69
  (4 shorter events, 0.1 us)
Async XLA Ops:
  7.2 176.8 %copy-start = (bf16[1,2048,256]{2,1,0:T(8,128)(2,1)S(1)}, bf16[1,2048,256]{2,1,0:T(8,128)(2,1)}, u32[]{:S(2)}) copy-start(bf16[1,2048,256]{2,1,0:T(8,128)(2,1)} %param.11) | copy-start | bytes 3145732
  7.2 163.9 %all-gather.3.cloned.1.call-start = ((), (), s32[]{:S(2)}) async-start(), calls=%async_computation.5 | async-start | bytes 7864320 | tf_op jit(solution)/shard_map/all_gather | solution.py:82
  183.9 3.1 copy-start.1
  183.9 3.1 copy-start.2
  202.2 9.2 %all-to-all-start.3 = ((bf16[4,1,192]{2,1,0:T(2,128)(2,1)}), bf16[4,1,192]{2,1,0:T(2,128)(2,1)S(1)}, u32[]{:S(2)}, u32[]{:S(2)}) async-start(bf16[4,1,192]{2,1,0:T(2,128)(2,1)} %convert_element_type.54), calls=%async_computation.3 | async-start | bytes 8192 | tf_op jit(solution)/shard_map/all_to_all | solution.py:48
  211.4 41.1 %all-to-all-start.1 = ((bf16[4,192,2048]{2,1,0:T(8,128)(2,1)}), bf16[4,192,2048]{2,1,0:T(8,128)(2,1)}, u32[]{:S(2)}, u32[]{:S(2)}) async-start(bf16[4,192,2048]{2,1,0:T(8,128)(2,1)} %bitcast.50), calls=%async_computation.1 | async-start | bytes 6291456 | tf_op jit(solution)/shard_map/all_to_all | solution.py:48
  252.5 23.3 %all-to-all-start.4 = ((f32[16,1,12]{2,1,0:T(1,128)}), f32[16,1,12]{2,1,0:T(1,128)S(1)}, u32[]{:S(2)}, u32[]{:S(2)}) async-start(f32[16,1,12]{2,1,0:T(1,128)} %bitcast.14), calls=%async_computation.4 | async-start | bytes 16384 | tf_op jit(solution)/shard_map/all_to_all | solution.py:48
  264.5 15.5 %copy-start.3 = (s32[1,128,8]{1,2,0:T(8,128)S(1)}, s32[1,128,8]{1,2,0:T(8,128)}, u32[]{:S(2)}) copy-start(s32[1,128,8]{1,2,0:T(8,128)} %param.9) | copy-start | bytes 12292
  264.5 15.5 %copy-start.4 = (f32[1,128,8]{1,2,0:T(8,128)S(1)}, f32[1,128,8]{1,2,0:T(8,128)}, u32[]{:S(2)}) copy-start(f32[1,128,8]{1,2,0:T(8,128)} %param.10) | copy-start | bytes 12292
  275.8 48.2 %all-to-all-start.2 = ((bf16[16,12,2048]{2,1,0:T(8,128)(2,1)}), bf16[16,12,2048]{2,1,0:T(8,128)(2,1)S(1)}, u32[]{:S(2)}, u32[]{:S(2)}) async-start(bf16[16,12,2048]{2,1,0:T(8,128)(2,1)} %reshape.51), calls=%async_computation.2 | async-start | bytes 2097152 | tf_op jit(solution)/shard_map/all_to_all | solution.py:48
  324.9 13.5 %collective-permute-start = (bf16[128,2048]{1,0:T(8,128)(2,1)S(1)}, bf16[128,2048]{1,0:T(8,128)(2,1)S(1)}, u32[]{:S(2)}, u32[]{:S(2)}) collective-permute-start(bf16[128,2048]{1,0:T(8,128)(2,1)S(1)} %fusion), channel_id=1, source_target_pairs={{64,0},{128,64},{192,128},{256,192},{320,256},{384,320},{448,384},... | collective-permute-start | bytes 1572872 | tf_op jit(solution)/shard_map/ppermute | solution.py:13
Sparse Core Ops, SparseCore 0:
  96.0 75.0 all-gather.2
